TPU v7x, 256 devices: a whole 4x4x8 slice. The times are simulated.
256 devices in a mesh: pipe: 8 (over x, core), dp: 32 (over z, y).
Axes of the slice: x: 4, y: 4, z: 8, core: 2. Of those that a mesh axis runs over, the one named last changes fastest.
Arguments:
- x_ckpt: bfloat16 [8, 2, 32, 512, 512], P('pipe', None, 'dp'), may hold values from -6 to 6
- top_cot: bfloat16 [2, 32, 512, 512], P(None, 'dp'), may hold values from -6 to 6
- skip_cot: bfloat16 [2, 32, 512, 512], P(None, 'dp'), may hold values from -6 to 6
- w_conv: bfloat16 [8, 512, 3, 1024], P('pipe', 'dp'), may hold values from -0.15625 to 0.15625
- w_mix: bfloat16 [8, 512, 1024], P('pipe', 'dp'), may hold values from -0.25 to 0.25
Outputs:
- cot_inputs: bfloat16 [8, 2, 32, 512, 512], P('pipe', None, 'dp')
- grad_conv: float32 [8, 512, 3, 1024], P('pipe', 'dp')
- grad_mix: float32 [8, 512, 1024], P('pipe', 'dp')
All inputs are finite; a program needn't handle non-finite values.
Results may differ from a plain program's by a relative error of at most 0.014.
Values may be sent and summed in bfloat16 or wider, within the bound.
A program may use at most 128 MiB of HBM per device.

v0:
```python
import jax
import jax.numpy as jnp
from jax import lax
from jax.sharding import PartitionSpec as P


def passed_along(value, axis, steps):
    count = lax.axis_size(axis)
    leading, last = (max(0, -steps), min(count, count - steps))
    return lax.ppermute(value, axis, [(source, source + steps) for source in range(leading, last)])


def delay_seq(signal, shift_by):
    samples = signal.shape[1]
    rolled = jnp.roll(signal, shift_by, axis=1)
    positions = lax.broadcasted_iota(jnp.int32, (1, samples, 1), 1)
    return jnp.where(positions >= shift_by, rolled, jnp.zeros_like(rolled))


def advance_seq(signal, shift_by):
    samples = signal.shape[1]
    rolled = jnp.roll(signal, -shift_by, axis=1)
    positions = lax.broadcasted_iota(jnp.int32, (1, samples, 1), 1)
    return jnp.where(positions < samples - shift_by, rolled, jnp.zeros_like(rolled))


def tap_stack(signal, dilation):
    return jnp.stack([delay_seq(signal, offset * dilation) for offset in range(3)], axis=2)


def layer_back(x_rows, grad_next, skip_grad, conv_w, mix_w, dilation):
    channels = x_rows.shape[2]
    tapped_x = tap_stack(x_rows, dilation)
    pre_act = jnp.einsum("slkc,ckn->sln", tapped_x, conv_w, preferred_element_type=jnp.float32)
    filter_act = jnp.tanh(pre_act[..., :channels])
    gate_act = jax.nn.sigmoid(pre_act[..., channels:])
    hidden = (filter_act * gate_act).astype(jnp.bfloat16)
    cot_pair = jnp.concatenate([grad_next, skip_grad], axis=2)
    hid_grad = jnp.einsum("sln,cn->slc", cot_pair, mix_w, preferred_element_type=jnp.float32)
    pre_grad = jnp.concatenate(
        [
            hid_grad * gate_act * (1.0 - filter_act * filter_act),
            hid_grad * filter_act * gate_act * (1.0 - gate_act),
        ],
        axis=2,
    ).astype(jnp.bfloat16)
    back_taps = jnp.einsum("sln,ckn->slkc", pre_grad, conv_w, preferred_element_type=jnp.float32)
    input_grad = grad_next.astype(jnp.float32)
    for offset in range(3):
        input_grad = input_grad + advance_seq(back_taps[:, :, offset], offset * dilation)
    return (input_grad.astype(jnp.bfloat16), tapped_x, hidden, pre_grad, cot_pair)


def weight_terms(tapped_x, hidden, pre_grad, cot_pair):
    conv_term = jnp.einsum("slkc,sln->ckn", tapped_x, pre_grad, preferred_element_type=jnp.float32)
    mix_term = jnp.einsum("slc,sln->cn", hidden, cot_pair, preferred_element_type=jnp.float32)
    return jnp.concatenate([conv_term.reshape(conv_term.shape[0], -1), mix_term], axis=1)


def local(x_ckpt, top_cot, skip_cot, w_conv, w_mix):
    sec_count = lax.axis_size("pipe")
    sec_index = lax.axis_index("pipe")
    dilation = jnp.left_shift(jnp.int32(1), sec_index)
    conv_full, mix_full = (
        lax.all_gather(w_conv, "dp", axis=1, tiled=True),
        lax.all_gather(w_mix, "dp", axis=1, tiled=True),
    )
    conv_w = conv_full[0]
    mix_w = mix_full[0]
    micro_count, seq_count, samples, channels = x_ckpt.shape[1:]
    all_rows = micro_count * seq_count
    x_rows = x_ckpt[0].reshape(all_rows, samples, channels)
    top_rows = top_cot.reshape(all_rows, samples, channels)
    skip_rows = skip_cot.reshape(all_rows, samples, channels)
    is_last = sec_index == sec_count - 1
    blk_count = all_rows // seq_count
    step_count = sec_count + blk_count - 1
    act_shape = (seq_count, samples, channels)
    pair_shape = (seq_count, samples, 2 * channels)
    grad_init = jnp.zeros((channels, 8 * channels), jnp.float32)
    hid_init = jnp.zeros((1,), jnp.bfloat16)
    pre_init = jnp.zeros((1,), jnp.bfloat16)
    pair_init = jnp.zeros((1,), jnp.bfloat16)

    def step_fn(step_no, state_tuple):
        received, cot_store, grad_acc, hid_store, pre_store, pair_store = state_tuple
        blk_index = step_no - (sec_count - 1 - sec_index)
        is_active = (blk_index >= 0) & (blk_index < blk_count)
        row_start = jnp.clip(blk_index, 0, blk_count - 1) * seq_count
        x_blk = lax.dynamic_slice_in_dim(x_rows, row_start, seq_count, 0)
        top_blk = lax.dynamic_slice_in_dim(top_rows, row_start, seq_count, 0)
        skip_blk = lax.dynamic_slice_in_dim(skip_rows, row_start, seq_count, 0)
        grad_next = jnp.where(is_last, top_blk, received)

        def do_work(unused):
            input_grad, tapped_x, hidden, pre_grad, cot_pair = layer_back(
                x_blk, grad_next, skip_blk, conv_w, mix_w, dilation
            )
            grad_term = weight_terms(tapped_x, hidden, pre_grad, cot_pair)
            return (input_grad, hidden, pre_grad, cot_pair, grad_term)

        def no_work(unused):
            return (
                jnp.zeros(act_shape, jnp.bfloat16),
                jnp.zeros(act_shape, jnp.bfloat16),
                jnp.zeros(pair_shape, jnp.bfloat16),
                jnp.zeros(pair_shape, jnp.bfloat16),
                jnp.zeros_like(grad_acc),
            )

        input_grad, hidden, pre_grad, cot_pair, grad_term = lax.cond(is_active, do_work, no_work, 0)
        grad_acc = grad_acc + grad_term
        cot_store = jnp.where(
            is_active,
            lax.dynamic_update_slice_in_dim(cot_store, input_grad, row_start, 0),
            cot_store,
        )
        received = passed_along(input_grad, "pipe", -1)
        return (received, cot_store, grad_acc, hid_store, pre_store, pair_store)

    initial = (
        jnp.zeros(act_shape, jnp.bfloat16),
        jnp.zeros((all_rows, samples, channels), jnp.bfloat16),
        grad_init,
        hid_init,
        pre_init,
        pair_init,
    )
    final_state = lax.fori_loop(0, step_count, step_fn, initial)
    cot_store, grad_acc, hid_store, pre_store, pair_store = final_state[1:]
    shard_rows = channels // lax.axis_size("dp")
    shares = lax.psum_scatter(grad_acc, "dp", scatter_dimension=0, tiled=True)
    conv_share = shares[:, : 6 * channels].reshape(shard_rows, 3, 2 * channels)
    mix_share = shares[:, 6 * channels :]
    return (
        cot_store.reshape(1, micro_count, seq_count, samples, channels),
        conv_share[None],
        mix_share[None],
    )


def solution(mesh):
    placed = (
        P("pipe", None, "dp", None, None),
        P(None, "dp", None, None),
        P(None, "dp", None, None),
        P("pipe", "dp", None, None),
        P("pipe", "dp", None),
    )
    return jax.shard_map(
        local,
        mesh=mesh,
        in_specs=placed,
        out_specs=(
            P("pipe", None, "dp", None, None),
            P("pipe", "dp", None, None),
            P("pipe", "dp", None),
        ),
        check_vma=False,
    )
```

profile of v0, /device:TPU:2, one launch (start us, length us, event | category | flops | bytes accessed | tf_op | source)
XLA Modules:
  0.0 634.7 jit_solution(10756008087756776390)
XLA Ops:
  8.7 81.3 %all-gather.3.cloned.1.call-done = bf16[1,512,1024]{2,1,0:T(8,128)(2,1)} async-done(((bf16[1,16,1024]{2,1,0:T(8,128)(2,1)}), bf16[1,512,1024]{2,1,0:T(8,128)(2,1)}) %all-gather.3.cloned.1.call-update) | async-done | bytes 1048592 | tf_op jit(solution)/shard_map/all_gather | solution.py:66
  90.0 79.5 %all-gather.5.cloned.1.call-done = bf16[1,512,3,1024]{3,1,2,0:T(8,128)(2,1)} async-done(((bf16[1,16,3,1024]{3,1,2,0:T(8,128)(2,1)}), bf16[1,512,3,1024]{3,1,2,0:T(8,128)(2,1)}) %all-gather.5.cloned.1.call-update) | async-done | bytes 3145744 | tf_op jit(solution)/shard_map/all_gather | solution.py:65
  170.6 218.1 %while.20 = (s32[]{:T(128)}, bf16[1,512,512]{2,1,0:T(8,128)(2,1)S(1)}, bf16[2,512,512]{2,1,0:T(8,128)(2,1)}, f32[512,4096]{0,1:T(8,128)}, s32[]{:T(128)}, /*inde...) while((s32[]{:T(128)}, ...), condition=%wide.region_3.8_spmd.clone, body=%wide.region_0.7_spmd.clone.sunk | while | flops 5937039872 | bytes 117971056 | solution.py:129
  170.6 4.3 conditional.3
  170.6 4.3 broadcast.78
  174.9 1.9 collective-permute-start
  176.8 8.8 %select_add_fusion.2 = f32[512,4096]{0,1:T(8,128)} fusion(f32[512,4096]{0,1:T(8,128)} %get-tuple-element.522, f32[512,4096]{0,1:T(8,128)} %get-tuple-element.545, pred[]{:T(512)S(6)} %compare.5), kind=kLoop, calls=%fused_computation.59.clone.1 | loop fusion | flops 4194304 | bytes 25165824 | tf_op jit(solution)/shard_map/while/body/eval_jaxpr/add | solution.py:112
  186.8 4.3 conditional.3
  186.9 4.3 broadcast.78
  191.2 2.5 collective-permute-start
  193.7 11.2 %select_add_fusion.2 = f32[512,4096]{0,1:T(8,128)} fusion(f32[512,4096]{0,1:T(8,128)} %get-tuple-element.522, f32[512,4096]{0,1:T(8,128)} %get-tuple-element.545, pred[]{:T(512)S(6)} %compare.5), kind=kLoop, calls=%fused_computation.59.clone.1 | loop fusion | flops 4194304 | bytes 25165824 | tf_op jit(solution)/shard_map/while/body/eval_jaxpr/add | solution.py:112
  206.1 4.3 conditional.3
  206.1 4.3 broadcast.78
  210.4 1.9 collective-permute-start
  212.4 11.2 %select_add_fusion.2 = f32[512,4096]{0,1:T(8,128)} fusion(f32[512,4096]{0,1:T(8,128)} %get-tuple-element.522, f32[512,4096]{0,1:T(8,128)} %get-tuple-element.545, pred[]{:T(512)S(6)} %compare.5), kind=kLoop, calls=%fused_computation.59.clone.1 | loop fusion | flops 4194304 | bytes 25165824 | tf_op jit(solution)/shard_map/while/body/eval_jaxpr/add | solution.py:112
  224.7 4.3 conditional.3
  224.8 4.3 broadcast.78
  229.1 1.9 collective-permute-start
  231.0 11.2 %select_add_fusion.2 = f32[512,4096]{0,1:T(8,128)} fusion(f32[512,4096]{0,1:T(8,128)} %get-tuple-element.522, f32[512,4096]{0,1:T(8,128)} %get-tuple-element.545, pred[]{:T(512)S(6)} %compare.5), kind=kLoop, calls=%fused_computation.59.clone.1 | loop fusion | flops 4194304 | bytes 25165824 | tf_op jit(solution)/shard_map/while/body/eval_jaxpr/add | solution.py:112
  243.4 4.3 conditional.3
  243.4 4.3 broadcast.78
  247.7 1.9 collective-permute-start
  249.7 11.2 %select_add_fusion.2 = f32[512,4096]{0,1:T(8,128)} fusion(f32[512,4096]{0,1:T(8,128)} %get-tuple-element.522, f32[512,4096]{0,1:T(8,128)} %get-tuple-element.545, pred[]{:T(512)S(6)} %compare.5), kind=kLoop, calls=%fused_computation.59.clone.1 | loop fusion | flops 4194304 | bytes 25165824 | tf_op jit(solution)/shard_map/while/body/eval_jaxpr/add | solution.py:112
  261.0 19.7 %collective-permute-done = bf16[1,512,512]{2,1,0:T(8,128)(2,1)S(1)} collective-permute-done((bf16[1,512,512]{2,1,0:T(8,128)(2,1)S(1)}, bf16[1,512,512]{2,1,0:T(8,128)(2,1)S(1)}, u32[]{:S(2)}, u32[]{:S(2)}) %collective-permute-start) | collective-permute-done | bytes 524320 | tf_op jit(solution)/shard_map/while/body/eval_jaxpr/ppermute | solution.py:10
  280.8 16.7 %conditional.3 = (bf16[1,512,512]{2,1,0:T(8,128)(2,1)S(1)}, f32[512,4096]{0,1:T(8,128)}) conditional(s32[]{:T(128)} %convert_element_type.39, () %tuple.71, (pred[]{:T(512)}, bf16[2,512,512]{2,1,0:T(8,128)(2,1)}, s32[]{:T(128)}, bf16[1,512,512]{2,1,0:T(8,128)(2,1)S(1)}, bf16[2,512,512]{2,1,0:T(8,128)(2,1)}, /*index=5*/bf16[512,1024]{1,0:T(8,128)(2,1)}, ...), branch_computations={%region_1.1_spmd, %region_2.6_spmd} | conditional | flops 5932583424 | bytes 80746224 | solution.py:111
  284.4 1.8 convolution_bitcast_fusion.1
  288.3 1.8 convolution_bitcast_fusion
  291.5 1.8 fusion.12
  293.3 4.2 pad_maximum_fusion
  297.5 1.9 collective-permute-start
  299.5 11.2 %select_add_fusion.2 = f32[512,4096]{0,1:T(8,128)} fusion(f32[512,4096]{0,1:T(8,128)} %get-tuple-element.522, f32[512,4096]{0,1:T(8,128)} %get-tuple-element.545, pred[]{:T(512)S(6)} %compare.5), kind=kLoop, calls=%fused_computation.59.clone.1 | loop fusion | flops 4194304 | bytes 25165824 | tf_op jit(solution)/shard_map/while/body/eval_jaxpr/add | solution.py:112
  311.8 16.7 %conditional.3 = (bf16[1,512,512]{2,1,0:T(8,128)(2,1)S(1)}, f32[512,4096]{0,1:T(8,128)}) conditional(s32[]{:T(128)} %convert_element_type.39, () %tuple.71, (pred[]{:T(512)}, bf16[2,512,512]{2,1,0:T(8,128)(2,1)}, s32[]{:T(128)}, bf16[1,512,512]{2,1,0:T(8,128)(2,1)S(1)}, bf16[2,512,512]{2,1,0:T(8,128)(2,1)}, /*index=5*/bf16[512,1024]{1,0:T(8,128)(2,1)}, ...), branch_computations={%region_1.1_spmd, %region_2.6_spmd} | conditional | flops 5932583424 | bytes 80746224 | solution.py:111
  315.4 1.8 convolution_bitcast_fusion.1
  319.3 1.8 convolution_bitcast_fusion
  322.5 1.8 fusion.12
  324.3 4.2 pad_maximum_fusion
  328.5 1.9 collective-permute-start
  330.5 11.2 %select_add_fusion.2 = f32[512,4096]{0,1:T(8,128)} fusion(f32[512,4096]{0,1:T(8,128)} %get-tuple-element.522, f32[512,4096]{0,1:T(8,128)} %get-tuple-element.545, pred[]{:T(512)S(6)} %compare.5), kind=kLoop, calls=%fused_computation.59.clone.1 | loop fusion | flops 4194304 | bytes 25165824 | tf_op jit(solution)/shard_map/while/body/eval_jaxpr/add | solution.py:112
  342.8 4.3 conditional.3
  342.9 4.3 broadcast.78
  347.2 10.5 %collective-permute-start = (bf16[1,512,512]{2,1,0:T(8,128)(2,1)S(1)}, bf16[1,512,512]{2,1,0:T(8,128)(2,1)S(1)}, u32[]{:S(2)}, u32[]{:S(2)}) collective-permute-start(bf16[1,512,512]{2,1,0:T(8,128)(2,1)S(1)} %get-tuple-element.521), channel_id=1, source_target_pairs={{32,0},{64,32},{96,64},{128,96},{160,128},{192,160},{224,192},{33,... | collective-permute-start | bytes 1572872 | tf_op jit(solution)/shard_map/while/body/eval_jaxpr/ppermute | solution.py:10
  357.7 11.2 %select_add_fusion.2 = f32[512,4096]{0,1:T(8,128)} fusion(f32[512,4096]{0,1:T(8,128)} %get-tuple-element.522, f32[512,4096]{0,1:T(8,128)} %get-tuple-element.545, pred[]{:T(512)S(6)} %compare.5), kind=kLoop, calls=%fused_computation.59.clone.1 | loop fusion | flops 4194304 | bytes 25165824 | tf_op jit(solution)/shard_map/while/body/eval_jaxpr/add | solution.py:112
  370.1 4.3 conditional.3
  370.1 4.3 broadcast.78
  374.4 1.9 collective-permute-start
  376.3 11.2 %select_add_fusion.2 = f32[512,4096]{0,1:T(8,128)} fusion(f32[512,4096]{0,1:T(8,128)} %get-tuple-element.522, f32[512,4096]{0,1:T(8,128)} %get-tuple-element.545, pred[]{:T(512)S(6)} %compare.5), kind=kLoop, calls=%fused_computation.59.clone.1 | loop fusion | flops 4194304 | bytes 25165824 | tf_op jit(solution)/shard_map/while/body/eval_jaxpr/add | solution.py:112
  388.7 8.9 %copy.15 = f32[512,4096]{1,0:T(8,128)} copy(f32[512,4096]{0,1:T(8,128)} %get-tuple-element.365) | data formatting | bytes 16777216 | tf_op jit(solution)/shard_map/while | solution.py:129
  397.6 227.2 %reduce-scatter.2.cloned.1.call-done = f32[16,4096]{1,0:T(8,128)} async-done(((f32[512,4096]{1,0:T(8,128)}), f32[16,4096]{1,0:T(8,128)}) %reduce-scatter.2.cloned.1.call-update) | async-done | bytes 262160 | tf_op jit(solution)/shard_map/reduce_scatter | solution.py:132
  (101 shorter events, 29.4 us)
Async XLA Ops:
  7.2 82.8 %all-gather.3.cloned.1.call-start = ((), (), s32[]{:S(2)}) async-start(), calls=%async_computation.1 | async-start | bytes 1081344 | tf_op jit(solution)/shard_map/all_gather | solution.py:66
  7.9 161.6 %all-gather.5.cloned.1.call-start = ((), (), s32[]{:S(2)}) async-start(), calls=%async_computation.2 | async-start | bytes 3244032 | tf_op jit(solution)/shard_map/all_gather | solution.py:65
  8.6 616.2 %reduce-scatter.2.cloned.1.call-start = ((), (), s32[]{:S(2)}) async-start(), calls=%async_computation.3 | async-start | bytes 8650752 | tf_op jit(solution)/shard_map/reduce_scatter | solution.py:132
  174.9 11.0 %collective-permute-start = (bf16[1,512,512]{2,1,0:T(8,128)(2,1)S(1)}, bf16[1,512,512]{2,1,0:T(8,128)(2,1)S(1)}, u32[]{:S(2)}, u32[]{:S(2)}) collective-permute-start(bf16[1,512,512]{2,1,0:T(8,128)(2,1)S(1)} %get-tuple-element.521), channel_id=1, source_target_pairs={{32,0},{64,32},{96,64},{128,96},{160,128},{192,160},{224,192},{33,... | collective-permute-start | bytes 1572872 | tf_op jit(solution)/shard_map/while/body/eval_jaxpr/ppermute | solution.py:10
  176.8 8.8 %copy-start = (bf16[2,512,512]{2,1,0:T(8,128)(2,1)S(1)}, bf16[2,512,512]{2,1,0:T(8,128)(2,1)}, u32[]{:S(2)}) copy-start(bf16[2,512,512]{2,1,0:T(8,128)(2,1)} %get-tuple-element.544) | copy-start | bytes 3145732 | tf_op jit(solution)/shard_map/while
  185.9 1.0 copy-start.1
  191.2 14.0 %collective-permute-start = (bf16[1,512,512]{2,1,0:T(8,128)(2,1)S(1)}, bf16[1,512,512]{2,1,0:T(8,128)(2,1)S(1)}, u32[]{:S(2)}, u32[]{:S(2)}) collective-permute-start(bf16[1,512,512]{2,1,0:T(8,128)(2,1)S(1)} %get-tuple-element.521), channel_id=1, source_target_pairs={{32,0},{64,32},{96,64},{128,96},{160,128},{192,160},{224,192},{33,... | collective-permute-start | bytes 1572872 | tf_op jit(solution)/shard_map/while/body/eval_jaxpr/ppermute | solution.py:10
  193.7 11.2 %copy-start = (bf16[2,512,512]{2,1,0:T(8,128)(2,1)S(1)}, bf16[2,512,512]{2,1,0:T(8,128)(2,1)}, u32[]{:S(2)}) copy-start(bf16[2,512,512]{2,1,0:T(8,128)(2,1)} %get-tuple-element.544) | copy-start | bytes 3145732 | tf_op jit(solution)/shard_map/while
  205.1 1.0 copy-start.1
  210.4 13.3 %collective-permute-start = (bf16[1,512,512]{2,1,0:T(8,128)(2,1)S(1)}, bf16[1,512,512]{2,1,0:T(8,128)(2,1)S(1)}, u32[]{:S(2)}, u32[]{:S(2)}) collective-permute-start(bf16[1,512,512]{2,1,0:T(8,128)(2,1)S(1)} %get-tuple-element.521), channel_id=1, source_target_pairs={{32,0},{64,32},{96,64},{128,96},{160,128},{192,160},{224,192},{33,... | collective-permute-start | bytes 1572872 | tf_op jit(solution)/shard_map/while/body/eval_jaxpr/ppermute | solution.py:10
  212.4 11.2 %copy-start = (bf16[2,512,512]{2,1,0:T(8,128)(2,1)S(1)}, bf16[2,512,512]{2,1,0:T(8,128)(2,1)}, u32[]{:S(2)}) copy-start(bf16[2,512,512]{2,1,0:T(8,128)(2,1)} %get-tuple-element.544) | copy-start | bytes 3145732 | tf_op jit(solution)/shard_map/while
  223.8 1.0 copy-start.1
  229.1 13.3 %collective-permute-start = (bf16[1,512,512]{2,1,0:T(8,128)(2,1)S(1)}, bf16[1,512,512]{2,1,0:T(8,128)(2,1)S(1)}, u32[]{:S(2)}, u32[]{:S(2)}) collective-permute-start(bf16[1,512,512]{2,1,0:T(8,128)(2,1)S(1)} %get-tuple-element.521), channel_id=1, source_target_pairs={{32,0},{64,32},{96,64},{128,96},{160,128},{192,160},{224,192},{33,... | collective-permute-start | bytes 1572872 | tf_op jit(solution)/shard_map/while/body/eval_jaxpr/ppermute | solution.py:10
  231.0 11.2 %copy-start = (bf16[2,512,512]{2,1,0:T(8,128)(2,1)S(1)}, bf16[2,512,512]{2,1,0:T(8,128)(2,1)}, u32[]{:S(2)}) copy-start(bf16[2,512,512]{2,1,0:T(8,128)(2,1)} %get-tuple-element.544) | copy-start | bytes 3145732 | tf_op jit(solution)/shard_map/while
  242.4 1.0 copy-start.1
  247.7 33.1 %collective-permute-start = (bf16[1,512,512]{2,1,0:T(8,128)(2,1)S(1)}, bf16[1,512,512]{2,1,0:T(8,128)(2,1)S(1)}, u32[]{:S(2)}, u32[]{:S(2)}) collective-permute-start(bf16[1,512,512]{2,1,0:T(8,128)(2,1)S(1)} %get-tuple-element.521), channel_id=1, source_target_pairs={{32,0},{64,32},{96,64},{128,96},{160,128},{192,160},{224,192},{33,... | collective-permute-start | bytes 1572872 | tf_op jit(solution)/shard_map/while/body/eval_jaxpr/ppermute | solution.py:10
  249.6 11.2 %copy-start = (bf16[2,512,512]{2,1,0:T(8,128)(2,1)S(1)}, bf16[2,512,512]{2,1,0:T(8,128)(2,1)}, u32[]{:S(2)}) copy-start(bf16[2,512,512]{2,1,0:T(8,128)(2,1)} %get-tuple-element.544) | copy-start | bytes 3145732 | tf_op jit(solution)/shard_map/while
  261.0 19.7 %copy-start.1 = (bf16[2,512,512]{2,1,0:T(8,128)(2,1)}, bf16[2,512,512]{2,1,0:T(8,128)(2,1)S(1)}, u32[]{:S(2)}) copy-start(bf16[2,512,512]{2,1,0:T(8,128)(2,1)S(1)} %select_dynamic-update-slice_fusion.2) | copy-start | bytes 3145732 | tf_op jit(solution)/shard_map/while
  280.8 3.6 copy-start.2
  284.4 1.9 copy-start.3
  297.5 14.3 %collective-permute-start = (bf16[1,512,512]{2,1,0:T(8,128)(2,1)S(1)}, bf16[1,512,512]{2,1,0:T(8,128)(2,1)S(1)}, u32[]{:S(2)}, u32[]{:S(2)}) collective-permute-start(bf16[1,512,512]{2,1,0:T(8,128)(2,1)S(1)} %get-tuple-element.521), channel_id=1, source_target_pairs={{32,0},{64,32},{96,64},{128,96},{160,128},{192,160},{224,192},{33,... | collective-permute-start | bytes 1572872 | tf_op jit(solution)/shard_map/while/body/eval_jaxpr/ppermute | solution.py:10
  299.4 11.2 %copy-start = (bf16[2,512,512]{2,1,0:T(8,128)(2,1)S(1)}, bf16[2,512,512]{2,1,0:T(8,128)(2,1)}, u32[]{:S(2)}) copy-start(bf16[2,512,512]{2,1,0:T(8,128)(2,1)} %get-tuple-element.544) | copy-start | bytes 3145732 | tf_op jit(solution)/shard_map/while
  310.8 1.0 copy-start.1
  311.8 3.6 copy-start.2
  315.4 1.9 copy-start.3
  328.5 13.3 %collective-permute-start = (bf16[1,512,512]{2,1,0:T(8,128)(2,1)S(1)}, bf16[1,512,512]{2,1,0:T(8,128)(2,1)S(1)}, u32[]{:S(2)}, u32[]{:S(2)}) collective-permute-start(bf16[1,512,512]{2,1,0:T(8,128)(2,1)S(1)} %get-tuple-element.521), channel_id=1, source_target_pairs={{32,0},{64,32},{96,64},{128,96},{160,128},{192,160},{224,192},{33,... | collective-permute-start | bytes 1572872 | tf_op jit(solution)/shard_map/while/body/eval_jaxpr/ppermute | solution.py:10
  330.5 11.2 %copy-start = (bf16[2,512,512]{2,1,0:T(8,128)(2,1)S(1)}, bf16[2,512,512]{2,1,0:T(8,128)(2,1)}, u32[]{:S(2)}) copy-start(bf16[2,512,512]{2,1,0:T(8,128)(2,1)} %get-tuple-element.544) | copy-start | bytes 3145732 | tf_op jit(solution)/shard_map/while
  341.9 1.0 copy-start.1
  347.2 21.9 %collective-permute-start = (bf16[1,512,512]{2,1,0:T(8,128)(2,1)S(1)}, bf16[1,512,512]{2,1,0:T(8,128)(2,1)S(1)}, u32[]{:S(2)}, u32[]{:S(2)}) collective-permute-start(bf16[1,512,512]{2,1,0:T(8,128)(2,1)S(1)} %get-tuple-element.521), channel_id=1, source_target_pairs={{32,0},{64,32},{96,64},{128,96},{160,128},{192,160},{224,192},{33,... | collective-permute-start | bytes 1572872 | tf_op jit(solution)/shard_map/while/body/eval_jaxpr/ppermute | solution.py:10
  357.7 11.2 %copy-start = (bf16[2,512,512]{2,1,0:T(8,128)(2,1)S(1)}, bf16[2,512,512]{2,1,0:T(8,128)(2,1)}, u32[]{:S(2)}) copy-start(bf16[2,512,512]{2,1,0:T(8,128)(2,1)} %get-tuple-element.544) | copy-start | bytes 3145732 | tf_op jit(solution)/shard_map/while
  369.1 1.0 copy-start.1
  374.4 13.3 %collective-permute-start = (bf16[1,512,512]{2,1,0:T(8,128)(2,1)S(1)}, bf16[1,512,512]{2,1,0:T(8,128)(2,1)S(1)}, u32[]{:S(2)}, u32[]{:S(2)}) collective-permute-start(bf16[1,512,512]{2,1,0:T(8,128)(2,1)S(1)} %get-tuple-element.521), channel_id=1, source_target_pairs={{32,0},{64,32},{96,64},{128,96},{160,128},{192,160},{224,192},{33,... | collective-permute-start | bytes 1572872 | tf_op jit(solution)/shard_map/while/body/eval_jaxpr/ppermute | solution.py:10
  376.3 11.2 %copy-start = (bf16[2,512,512]{2,1,0:T(8,128)(2,1)S(1)}, bf16[2,512,512]{2,1,0:T(8,128)(2,1)}, u32[]{:S(2)}) copy-start(bf16[2,512,512]{2,1,0:T(8,128)(2,1)} %get-tuple-element.544) | copy-start | bytes 3145732 | tf_op jit(solution)/shard_map/while
  387.7 1.0 copy-start.1
Sparse Core Ops, SparseCore 0:
  10.6 79.3 all-gather.2
  92.6 76.8 all-gather.4
  397.8 227.0 reduce-scatter.1
where the time goes:
time: 635 us
  waiting for transfers between devices  410 us (65%)
  other arithmetic  116 us (18%)
  local copies, waits for them, and re-layouts  53.3 us (8%)
  starting transfers between devices  26.5 us (4%)
  matrix products  14.9 us (2%)
  between operations  13.8 us (2%)
    reduce_scatter x1, waiting for transfers between devices, local(): shares = lax.psum_scatter(grad_acc, 'dp', scatter_dimension=0, tiled=True)  227 us
    add x9, other arithmetic, step_fn(): grad_acc = grad_acc + grad_term  98.4 us
    all_gather x1, waiting for transfers between devices, local(): lax.all_gather(w_mix, 'dp', axis=1, tiled=True)  81.3 us
    all_gather x1, waiting for transfers between devices, local(): lax.all_gather(w_conv, 'dp', axis=1, tiled=True)  79.5 us
    another operation x15, local copies, waits for them, and re-layouts  30.4 us
    ppermute x9, starting transfers between devices, passed_along(): lax.ppermute(value, axis, [(source, source + steps) for source in range(l...  26.4 us
    ppermute x9, waiting for transfers between devices, passed_along(): lax.ppermute(value, axis, [(source, source + steps) for source in range(l...  20.7 us
  transfers between devices with their start and end apart: 12, of which 5 were waited for; matrix products, arithmetic and copies ran while one was open for 16% of the time, Pallas kernels for 0%

commit v1 on v0

--- a/solution.py
+++ b/solution.py
@@ -62,7 +62,9 @@
     sec_index = lax.axis_index("pipe")
     dilation = jnp.left_shift(jnp.int32(1), sec_index)
     conv_full, mix_full = (
-        lax.all_gather(w_conv, "dp", axis=1, tiled=True),
+        jnp.concatenate(
+            lax.all_to_all(jnp.stack([w_conv] * lax.axis_size("dp"), axis=0), "dp", 0, 0), axis=1
+        ),
         lax.all_gather(w_mix, "dp", axis=1, tiled=True),
     )
     conv_w = conv_full[0]

time: 635 us -> 577 us (0.909)
  waiting for transfers between devices: 410 us -> 333 us
  starting transfers between devices: 26.5 us -> 38 us
  local copies, waits for them, and re-layouts: 53.3 us -> 60.5 us
    all_gather x1 -> x0, waiting for transfers between devices: 79.5 us -> none  [local(): lax.all_gather(w_conv, 'dp', axis=1, tiled=True)]
    all_to_all x0 -> x1, waiting for transfers between devices: none -> 76.1 us  [local(): lax.all_to_all(jnp.stack([w_conv] * lax.axis_size('dp'), axis=0), 'dp', 0...]
    all_gather x1, waiting for transfers between devices: 81.3 us -> 7.24 us  [local(): lax.all_gather(w_mix, 'dp', axis=1, tiled=True)]
    all_to_all x0 -> x1, starting transfers between devices: none -> 11.6 us  [local(): lax.all_to_all(jnp.stack([w_conv] * lax.axis_size('dp'), axis=0), 'dp', 0...]
    another operation x15 -> x16, local copies, waits for them, and re-layouts: 30.4 us -> 33.5 us
  transfers between devices with their start and end apart: 12 -> 12, of which waited for: 5 -> 5; matrix products, arithmetic and copies ran while one was open for 16% -> 18% of each run, Pallas kernels for 0% -> 0%
where the time goes in v1:
time: 577 us
  waiting for transfers between devices  333 us (58%)
  other arithmetic  116 us (20%)
  local copies, waits for them, and re-layouts  60.5 us (10%)
  starting transfers between devices  38 us (7%)
  matrix products  15 us (3%)
  between operations  14.1 us (2%)
    reduce_scatter x1, waiting for transfers between devices, local(): shares = lax.psum_scatter(grad_acc, 'dp', scatter_dimension=0, tiled=True)  228 us
    add x9, other arithmetic, step_fn(): grad_acc = grad_acc + grad_term  98.5 us
    all_to_all x1, waiting for transfers between devices, local(): lax.all_to_all(jnp.stack([w_conv] * lax.axis_size('dp'), axis=0), 'dp', 0...  76.1 us
    another operation x15, local copies, waits for them, and re-layouts  30.5 us
    ppermute x9, starting transfers between devices, passed_along(): lax.ppermute(value, axis, [(source, source + steps) for source in range(l...  26.3 us
    ppermute x9, waiting for transfers between devices, passed_along(): lax.ppermute(value, axis, [(source, source + steps) for source in range(l...  20.9 us
    all_to_all x1, starting transfers between devices, local(): lax.all_to_all(jnp.stack([w_conv] * lax.axis_size('dp'), axis=0), 'dp', 0...  11.6 us
  transfers between devices with their start and end apart: 12, of which 5 were waited for; matrix products, arithmetic and copies ran while one was open for 18% of the time, Pallas kernels for 0%

profile of v1, /device:TPU:2, one launch (start us, length us, event | category | flops | bytes accessed | tf_op | source)
XLA Modules:
  0.0 576.8 jit_solution(16075663190200414000)
XLA Ops:
  7.2 3.0 stack.18
  10.2 11.6 %all-to-all-start = ((bf16[32,1,16,3,1024]{4,2,3,1,0:T(8,128)(2,1)}), bf16[32,1,16,3,1024]{4,2,3,1,0:T(8,128)(2,1)}, u32[]{:S(2)}, u32[]{:S(2)}) async-start(bf16[32,1,16,3,1024]{4,2,3,1,0:T(8,128)(2,1)} %stack.18), calls=%async_computation | async-start | bytes 6291456 | tf_op jit(solution)/shard_map/all_to_all | solution.py:66
  22.6 76.1 %all-to-all-done = bf16[32,1,16,3,1024]{4,2,3,1,0:T(8,128)(2,1)} async-done(((bf16[32,1,16,3,1024]{4,2,3,1,0:T(8,128)(2,1)}), bf16[32,1,16,3,1024]{4,2,3,1,0:T(8,128)(2,1)}, u32[]{:S(2)}, u32[]{:S(2)}) %all-to-all-start) | async-done | bytes 3145760 | tf_op jit(solution)/shard_map/all_to_all | solution.py:66
  98.7 4.1 copy.25
  102.8 7.2 %all-gather.2.cloned.1.call-done = bf16[1,512,1024]{2,1,0:T(8,128)(2,1)} async-done(((bf16[1,16,1024]{2,1,0:T(8,128)(2,1)}), bf16[1,512,1024]{2,1,0:T(8,128)(2,1)}) %all-gather.2.cloned.1.call-update) | async-done | bytes 1048592 | tf_op jit(solution)/shard_map/all_gather | solution.py:68
  111.2 218.4 %while.20 = (s32[]{:T(128)}, bf16[1,512,512]{2,1,0:T(8,128)(2,1)S(1)}, bf16[2,512,512]{2,1,0:T(8,128)(2,1)}, f32[512,4096]{0,1:T(8,128)}, s32[]{:T(128)}, /*inde...) while((s32[]{:T(128)}, ...), condition=%wide.region_3.8_spmd.clone, body=%wide.region_0.7_spmd.clone.sunk | while | flops 5937039872 | bytes 117971056 | solution.py:131
  111.2 4.4 conditional.3
  111.2 4.3 broadcast.81
  115.5 1.9 collective-permute-start
  117.4 8.8 %select_add_fusion.2 = f32[512,4096]{0,1:T(8,128)} fusion(f32[512,4096]{0,1:T(8,128)} %get-tuple-element.528, f32[512,4096]{0,1:T(8,128)} %get-tuple-element.551, pred[]{:T(512)S(6)} %compare.5), kind=kLoop, calls=%fused_computation.59.clone.1 | loop fusion | flops 4194304 | bytes 25165824 | tf_op jit(solution)/shard_map/while/body/eval_jaxpr/add | solution.py:114
  127.4 4.4 conditional.3
  127.5 4.3 broadcast.81
  131.8 2.4 collective-permute-start
  134.2 11.2 %select_add_fusion.2 = f32[512,4096]{0,1:T(8,128)} fusion(f32[512,4096]{0,1:T(8,128)} %get-tuple-element.528, f32[512,4096]{0,1:T(8,128)} %get-tuple-element.551, pred[]{:T(512)S(6)} %compare.5), kind=kLoop, calls=%fused_computation.59.clone.1 | loop fusion | flops 4194304 | bytes 25165824 | tf_op jit(solution)/shard_map/while/body/eval_jaxpr/add | solution.py:114
  146.6 4.4 conditional.3
  146.6 4.3 broadcast.81
  150.9 1.9 collective-permute-start
  152.9 11.2 %select_add_fusion.2 = f32[512,4096]{0,1:T(8,128)} fusion(f32[512,4096]{0,1:T(8,128)} %get-tuple-element.528, f32[512,4096]{0,1:T(8,128)} %get-tuple-element.551, pred[]{:T(512)S(6)} %compare.5), kind=kLoop, calls=%fused_computation.59.clone.1 | loop fusion | flops 4194304 | bytes 25165824 | tf_op jit(solution)/shard_map/while/body/eval_jaxpr/add | solution.py:114
  165.2 4.4 conditional.3
  165.3 4.3 broadcast.81
  169.6 1.9 collective-permute-start
  171.5 11.2 %select_add_fusion.2 = f32[512,4096]{0,1:T(8,128)} fusion(f32[512,4096]{0,1:T(8,128)} %get-tuple-element.528, f32[512,4096]{0,1:T(8,128)} %get-tuple-element.551, pred[]{:T(512)S(6)} %compare.5), kind=kLoop, calls=%fused_computation.59.clone.1 | loop fusion | flops 4194304 | bytes 25165824 | tf_op jit(solution)/shard_map/while/body/eval_jaxpr/add | solution.py:114
  183.9 4.4 conditional.3
  183.9 4.3 broadcast.81
  188.2 1.9 collective-permute-start
  190.2 11.2 %select_add_fusion.2 = f32[512,4096]{0,1:T(8,128)} fusion(f32[512,4096]{0,1:T(8,128)} %get-tuple-element.528, f32[512,4096]{0,1:T(8,128)} %get-tuple-element.551, pred[]{:T(512)S(6)} %compare.5), kind=kLoop, calls=%fused_computation.59.clone.1 | loop fusion | flops 4194304 | bytes 25165824 | tf_op jit(solution)/shard_map/while/body/eval_jaxpr/add | solution.py:114
  201.6 20.0 %collective-permute-done = bf16[1,512,512]{2,1,0:T(8,128)(2,1)S(1)} collective-permute-done((bf16[1,512,512]{2,1,0:T(8,128)(2,1)S(1)}, bf16[1,512,512]{2,1,0:T(8,128)(2,1)S(1)}, u32[]{:S(2)}, u32[]{:S(2)}) %collective-permute-start) | collective-permute-done | bytes 524320 | tf_op jit(solution)/shard_map/while/body/eval_jaxpr/ppermute | solution.py:10
  221.6 16.8 %conditional.3 = (bf16[1,512,512]{2,1,0:T(8,128)(2,1)S(1)}, f32[512,4096]{0,1:T(8,128)}) conditional(s32[]{:T(128)} %convert_element_type.39, () %tuple.73, (pred[]{:T(512)}, bf16[2,512,512]{2,1,0:T(8,128)(2,1)}, s32[]{:T(128)}, bf16[1,512,512]{2,1,0:T(8,128)(2,1)S(1)}, bf16[2,512,512]{2,1,0:T(8,128)(2,1)}, /*index=5*/bf16[512,1024]{1,0:T(8,128)(2,1)}, ...), branch_computations={%region_1.1_spmd, %region_2.6_spmd} | conditional | flops 5932583424 | bytes 80746224 | solution.py:113
  225.2 1.8 convolution_bitcast_fusion.1
  229.1 1.9 convolution_bitcast_fusion
  234.1 4.2 pad_maximum_fusion
  238.3 1.9 collective-permute-start
  240.3 11.2 %select_add_fusion.2 = f32[512,4096]{0,1:T(8,128)} fusion(f32[512,4096]{0,1:T(8,128)} %get-tuple-element.528, f32[512,4096]{0,1:T(8,128)} %get-tuple-element.551, pred[]{:T(512)S(6)} %compare.5), kind=kLoop, calls=%fused_computation.59.clone.1 | loop fusion | flops 4194304 | bytes 25165824 | tf_op jit(solution)/shard_map/while/body/eval_jaxpr/add | solution.py:114
  252.6 16.8 %conditional.3 = (bf16[1,512,512]{2,1,0:T(8,128)(2,1)S(1)}, f32[512,4096]{0,1:T(8,128)}) conditional(s32[]{:T(128)} %convert_element_type.39, () %tuple.73, (pred[]{:T(512)}, bf16[2,512,512]{2,1,0:T(8,128)(2,1)}, s32[]{:T(128)}, bf16[1,512,512]{2,1,0:T(8,128)(2,1)S(1)}, bf16[2,512,512]{2,1,0:T(8,128)(2,1)}, /*index=5*/bf16[512,1024]{1,0:T(8,128)(2,1)}, ...), branch_computations={%region_1.1_spmd, %region_2.6_spmd} | conditional | flops 5932583424 | bytes 80746224 | solution.py:113
  260.1 1.9 convolution_bitcast_fusion
  265.2 4.2 pad_maximum_fusion
  269.4 1.9 collective-permute-start
  271.3 11.2 %select_add_fusion.2 = f32[512,4096]{0,1:T(8,128)} fusion(f32[512,4096]{0,1:T(8,128)} %get-tuple-element.528, f32[512,4096]{0,1:T(8,128)} %get-tuple-element.551, pred[]{:T(512)S(6)} %compare.5), kind=kLoop, calls=%fused_computation.59.clone.1 | loop fusion | flops 4194304 | bytes 25165824 | tf_op jit(solution)/shard_map/while/body/eval_jaxpr/add | solution.py:114
  283.7 4.4 conditional.3
  283.7 4.3 broadcast.81
  288.0 10.5 %collective-permute-start = (bf16[1,512,512]{2,1,0:T(8,128)(2,1)S(1)}, bf16[1,512,512]{2,1,0:T(8,128)(2,1)S(1)}, u32[]{:S(2)}, u32[]{:S(2)}) collective-permute-start(bf16[1,512,512]{2,1,0:T(8,128)(2,1)S(1)} %get-tuple-element.527), channel_id=1, source_target_pairs={{32,0},{64,32},{96,64},{128,96},{160,128},{192,160},{224,192},{33,... | collective-permute-start | bytes 1572872 | tf_op jit(solution)/shard_map/while/body/eval_jaxpr/ppermute | solution.py:10
  298.6 11.2 %select_add_fusion.2 = f32[512,4096]{0,1:T(8,128)} fusion(f32[512,4096]{0,1:T(8,128)} %get-tuple-element.528, f32[512,4096]{0,1:T(8,128)} %get-tuple-element.551, pred[]{:T(512)S(6)} %compare.5), kind=kLoop, calls=%fused_computation.59.clone.1 | loop fusion | flops 4194304 | bytes 25165824 | tf_op jit(solution)/shard_map/while/body/eval_jaxpr/add | solution.py:114
  311.0 4.4 conditional.3
  311.0 4.3 broadcast.81
  315.3 1.9 collective-permute-start
  317.2 11.2 %select_add_fusion.2 = f32[512,4096]{0,1:T(8,128)} fusion(f32[512,4096]{0,1:T(8,128)} %get-tuple-element.528, f32[512,4096]{0,1:T(8,128)} %get-tuple-element.551, pred[]{:T(512)S(6)} %compare.5), kind=kLoop, calls=%fused_computation.59.clone.1 | loop fusion | flops 4194304 | bytes 25165824 | tf_op jit(solution)/shard_map/while/body/eval_jaxpr/add | solution.py:114
  329.6 8.9 %copy.26 = f32[512,4096]{1,0:T(8,128)} copy(f32[512,4096]{0,1:T(8,128)} %get-tuple-element.365) | data formatting | bytes 16777216 | tf_op jit(solution)/shard_map/while | solution.py:131
  338.5 228.1 %reduce-scatter.2.cloned.1.call-done = f32[16,4096]{1,0:T(8,128)} async-done(((f32[512,4096]{1,0:T(8,128)}), f32[16,4096]{1,0:T(8,128)}) %reduce-scatter.2.cloned.1.call-update) | async-done | bytes 262160 | tf_op jit(solution)/shard_map/reduce_scatter | solution.py:134
  (102 shorter events, 34.1 us)
Async XLA Ops:
  10.2 88.5 %all-to-all-start = ((bf16[32,1,16,3,1024]{4,2,3,1,0:T(8,128)(2,1)}), bf16[32,1,16,3,1024]{4,2,3,1,0:T(8,128)(2,1)}, u32[]{:S(2)}, u32[]{:S(2)}) async-start(bf16[32,1,16,3,1024]{4,2,3,1,0:T(8,128)(2,1)} %stack.18), calls=%async_computation | async-start | bytes 6291456 | tf_op jit(solution)/shard_map/all_to_all | solution.py:66
  21.8 88.3 %all-gather.2.cloned.1.call-start = ((), (), s32[]{:S(2)}) async-start(), calls=%async_computation.2 | async-start | bytes 1081344 | tf_op jit(solution)/shard_map/all_gather | solution.py:68
  22.5 544.1 %reduce-scatter.2.cloned.1.call-start = ((), (), s32[]{:S(2)}) async-start(), calls=%async_computation.3 | async-start | bytes 8650752 | tf_op jit(solution)/shard_map/reduce_scatter | solution.py:134
  115.5 11.0 %collective-permute-start = (bf16[1,512,512]{2,1,0:T(8,128)(2,1)S(1)}, bf16[1,512,512]{2,1,0:T(8,128)(2,1)S(1)}, u32[]{:S(2)}, u32[]{:S(2)}) collective-permute-start(bf16[1,512,512]{2,1,0:T(8,128)(2,1)S(1)} %get-tuple-element.527), channel_id=1, source_target_pairs={{32,0},{64,32},{96,64},{128,96},{160,128},{192,160},{224,192},{33,... | collective-permute-start | bytes 1572872 | tf_op jit(solution)/shard_map/while/body/eval_jaxpr/ppermute | solution.py:10
  117.4 8.9 %copy-start = (bf16[2,512,512]{2,1,0:T(8,128)(2,1)S(1)}, bf16[2,512,512]{2,1,0:T(8,128)(2,1)}, u32[]{:S(2)}) copy-start(bf16[2,512,512]{2,1,0:T(8,128)(2,1)} %get-tuple-element.550) | copy-start | bytes 3145732 | tf_op jit(solution)/shard_map/while
  126.5 1.0 copy-start.1
  131.8 13.8 %collective-permute-start = (bf16[1,512,512]{2,1,0:T(8,128)(2,1)S(1)}, bf16[1,512,512]{2,1,0:T(8,128)(2,1)S(1)}, u32[]{:S(2)}, u32[]{:S(2)}) collective-permute-start(bf16[1,512,512]{2,1,0:T(8,128)(2,1)S(1)} %get-tuple-element.527), channel_id=1, source_target_pairs={{32,0},{64,32},{96,64},{128,96},{160,128},{192,160},{224,192},{33,... | collective-permute-start | bytes 1572872 | tf_op jit(solution)/shard_map/while/body/eval_jaxpr/ppermute | solution.py:10
  134.2 11.2 %copy-start = (bf16[2,512,512]{2,1,0:T(8,128)(2,1)S(1)}, bf16[2,512,512]{2,1,0:T(8,128)(2,1)}, u32[]{:S(2)}) copy-start(bf16[2,512,512]{2,1,0:T(8,128)(2,1)} %get-tuple-element.550) | copy-start | bytes 3145732 | tf_op jit(solution)/shard_map/while
  145.6 1.0 copy-start.1
  150.9 13.3 %collective-permute-start = (bf16[1,512,512]{2,1,0:T(8,128)(2,1)S(1)}, bf16[1,512,512]{2,1,0:T(8,128)(2,1)S(1)}, u32[]{:S(2)}, u32[]{:S(2)}) collective-permute-start(bf16[1,512,512]{2,1,0:T(8,128)(2,1)S(1)} %get-tuple-element.527), channel_id=1, source_target_pairs={{32,0},{64,32},{96,64},{128,96},{160,128},{192,160},{224,192},{33,... | collective-permute-start | bytes 1572872 | tf_op jit(solution)/shard_map/while/body/eval_jaxpr/ppermute | solution.py:10
  152.9 11.2 %copy-start = (bf16[2,512,512]{2,1,0:T(8,128)(2,1)S(1)}, bf16[2,512,512]{2,1,0:T(8,128)(2,1)}, u32[]{:S(2)}) copy-start(bf16[2,512,512]{2,1,0:T(8,128)(2,1)} %get-tuple-element.550) | copy-start | bytes 3145732 | tf_op jit(solution)/shard_map/while
  164.3 1.0 copy-start.1
  169.6 13.3 %collective-permute-start = (bf16[1,512,512]{2,1,0:T(8,128)(2,1)S(1)}, bf16[1,512,512]{2,1,0:T(8,128)(2,1)S(1)}, u32[]{:S(2)}, u32[]{:S(2)}) collective-permute-start(bf16[1,512,512]{2,1,0:T(8,128)(2,1)S(1)} %get-tuple-element.527), channel_id=1, source_target_pairs={{32,0},{64,32},{96,64},{128,96},{160,128},{192,160},{224,192},{33,... | collective-permute-start | bytes 1572872 | tf_op jit(solution)/shard_map/while/body/eval_jaxpr/ppermute | solution.py:10
  171.5 11.2 %copy-start = (bf16[2,512,512]{2,1,0:T(8,128)(2,1)S(1)}, bf16[2,512,512]{2,1,0:T(8,128)(2,1)}, u32[]{:S(2)}) copy-start(bf16[2,512,512]{2,1,0:T(8,128)(2,1)} %get-tuple-element.550) | copy-start | bytes 3145732 | tf_op jit(solution)/shard_map/while
  182.9 1.0 copy-start.1
  188.2 33.3 %collective-permute-start = (bf16[1,512,512]{2,1,0:T(8,128)(2,1)S(1)}, bf16[1,512,512]{2,1,0:T(8,128)(2,1)S(1)}, u32[]{:S(2)}, u32[]{:S(2)}) collective-permute-start(bf16[1,512,512]{2,1,0:T(8,128)(2,1)S(1)} %get-tuple-element.527), channel_id=1, source_target_pairs={{32,0},{64,32},{96,64},{128,96},{160,128},{192,160},{224,192},{33,... | collective-permute-start | bytes 1572872 | tf_op jit(solution)/shard_map/while/body/eval_jaxpr/ppermute | solution.py:10
  190.1 11.2 %copy-start = (bf16[2,512,512]{2,1,0:T(8,128)(2,1)S(1)}, bf16[2,512,512]{2,1,0:T(8,128)(2,1)}, u32[]{:S(2)}) copy-start(bf16[2,512,512]{2,1,0:T(8,128)(2,1)} %get-tuple-element.550) | copy-start | bytes 3145732 | tf_op jit(solution)/shard_map/while
  201.6 20.0 %copy-start.1 = (bf16[2,512,512]{2,1,0:T(8,128)(2,1)}, bf16[2,512,512]{2,1,0:T(8,128)(2,1)S(1)}, u32[]{:S(2)}) copy-start(bf16[2,512,512]{2,1,0:T(8,128)(2,1)S(1)} %select_dynamic-update-slice_fusion.2) | copy-start | bytes 3145732 | tf_op jit(solution)/shard_map/while
  221.6 3.6 copy-start.2
  225.2 1.9 copy-start.3
  238.3 14.3 %collective-permute-start = (bf16[1,512,512]{2,1,0:T(8,128)(2,1)S(1)}, bf16[1,512,512]{2,1,0:T(8,128)(2,1)S(1)}, u32[]{:S(2)}, u32[]{:S(2)}) collective-permute-start(bf16[1,512,512]{2,1,0:T(8,128)(2,1)S(1)} %get-tuple-element.527), channel_id=1, source_target_pairs={{32,0},{64,32},{96,64},{128,96},{160,128},{192,160},{224,192},{33,... | collective-permute-start | bytes 1572872 | tf_op jit(solution)/shard_map/while/body/eval_jaxpr/ppermute | solution.py:10
  240.2 11.2 %copy-start = (bf16[2,512,512]{2,1,0:T(8,128)(2,1)S(1)}, bf16[2,512,512]{2,1,0:T(8,128)(2,1)}, u32[]{:S(2)}) copy-start(bf16[2,512,512]{2,1,0:T(8,128)(2,1)} %get-tuple-element.550) | copy-start | bytes 3145732 | tf_op jit(solution)/shard_map/while
  251.7 1.0 copy-start.1
  252.6 3.6 copy-start.2
  256.2 1.9 copy-start.3
  269.4 13.3 %collective-permute-start = (bf16[1,512,512]{2,1,0:T(8,128)(2,1)S(1)}, bf16[1,512,512]{2,1,0:T(8,128)(2,1)S(1)}, u32[]{:S(2)}, u32[]{:S(2)}) collective-permute-start(bf16[1,512,512]{2,1,0:T(8,128)(2,1)S(1)} %get-tuple-element.527), channel_id=1, source_target_pairs={{32,0},{64,32},{96,64},{128,96},{160,128},{192,160},{224,192},{33,... | collective-permute-start | bytes 1572872 | tf_op jit(solution)/shard_map/while/body/eval_jaxpr/ppermute | solution.py:10
  271.3 11.2 %copy-start = (bf16[2,512,512]{2,1,0:T(8,128)(2,1)S(1)}, bf16[2,512,512]{2,1,0:T(8,128)(2,1)}, u32[]{:S(2)}) copy-start(bf16[2,512,512]{2,1,0:T(8,128)(2,1)} %get-tuple-element.550) | copy-start | bytes 3145732 | tf_op jit(solution)/shard_map/while
  282.7 1.0 copy-start.1
  288.0 22.0 %collective-permute-start = (bf16[1,512,512]{2,1,0:T(8,128)(2,1)S(1)}, bf16[1,512,512]{2,1,0:T(8,128)(2,1)S(1)}, u32[]{:S(2)}, u32[]{:S(2)}) collective-permute-start(bf16[1,512,512]{2,1,0:T(8,128)(2,1)S(1)} %get-tuple-element.527), channel_id=1, source_target_pairs={{32,0},{64,32},{96,64},{128,96},{160,128},{192,160},{224,192},{33,... | collective-permute-start | bytes 1572872 | tf_op jit(solution)/shard_map/while/body/eval_jaxpr/ppermute | solution.py:10
  298.6 11.2 %copy-start = (bf16[2,512,512]{2,1,0:T(8,128)(2,1)S(1)}, bf16[2,512,512]{2,1,0:T(8,128)(2,1)}, u32[]{:S(2)}) copy-start(bf16[2,512,512]{2,1,0:T(8,128)(2,1)} %get-tuple-element.550) | copy-start | bytes 3145732 | tf_op jit(solution)/shard_map/while
  310.0 1.0 copy-start.1
  315.3 13.3 %collective-permute-start = (bf16[1,512,512]{2,1,0:T(8,128)(2,1)S(1)}, bf16[1,512,512]{2,1,0:T(8,128)(2,1)S(1)}, u32[]{:S(2)}, u32[]{:S(2)}) collective-permute-start(bf16[1,512,512]{2,1,0:T(8,128)(2,1)S(1)} %get-tuple-element.527), channel_id=1, source_target_pairs={{32,0},{64,32},{96,64},{128,96},{160,128},{192,160},{224,192},{33,... | collective-permute-start | bytes 1572872 | tf_op jit(solution)/shard_map/while/body/eval_jaxpr/ppermute | solution.py:10
  317.2 11.2 %copy-start = (bf16[2,512,512]{2,1,0:T(8,128)(2,1)S(1)}, bf16[2,512,512]{2,1,0:T(8,128)(2,1)}, u32[]{:S(2)}) copy-start(bf16[2,512,512]{2,1,0:T(8,128)(2,1)} %get-tuple-element.550) | copy-start | bytes 3145732 | tf_op jit(solution)/shard_map/while
  328.6 1.0 copy-start.1
Sparse Core Ops, SparseCore 0:
  25.2 84.8 all-gather.1
  338.7 227.8 reduce-scatter.1
